TPU v7x, 256 devices: a whole 4x4x8 slice. The times are simulated.
256 devices in a mesh: grp: 4 (over x), tp: 32 (over y_lo, z, core), cores: 2 (over y_hi).
Axes of the slice: x: 4, y: 4 (y_hi: 2, y_lo: 2; y = y_hi * 2 + y_lo), z: 8, core: 2. Of those that a mesh axis runs over, the one named last changes fastest.
Arguments:
- tokens: bfloat16 [4096, 8192], P('grp', ('tp', 'cores')), may hold values from -6 to 6
- gate_up_weight: bfloat16 [8192, 2, 16384], P(None, None, ('tp', 'cores')), may hold values from -0.0625 to 0.0625
- down_factor_pool: bfloat16 [64, 8192, 256], P(('tp', 'cores'), 'grp'), may hold values from -0.0625 to 0.0625
- up_factor_pool: bfloat16 [64, 4, 64, 128, 128], P(('tp', 'cores'), 'grp'), may hold values from -0.5 to 0.5
- segment_adapters: int32 [4, 3], replicated, may hold values from 0 to 63
- segment_tile_counts: int32 [4, 3], P('grp'), may hold values from 1 to 4, 8 in all within a row
- adapter_pool_rows: int32 [64], replicated, may hold values from 0 to 63, each once
Outputs:
- hidden: bfloat16 [4096, 16384], P('grp', ('tp', 'cores'))
Inputs may be any that keep to these rules, and one draw needn't show every extreme that they name: `segment_tile_counts`: each row sums to 8. `adapter_pool_rows`: each pool row appears once.
All inputs are finite; a program needn't handle non-finite values.
Results may differ from a plain program's by a relative error of at most 0.0036.
Values may be sent and summed in bfloat16 or wider, within the bound.
No kernel may reach another device: no remote copies, remote signals or barrier semaphores. Data moves between devices by JAX's collectives and lax.ppermute only.
A program may use at most 192 MiB of HBM per device.

v0:
```python
import jax
import jax.numpy as jnp
from jax import lax
from jax.sharding import PartitionSpec as P

TILE = 128
adapter_scale = 0.5


def tile_segments(tile_lengths, tile_count):
    bounds = jnp.cumsum(tile_lengths)
    positions = jnp.arange(tile_count, dtype=jnp.int32)
    return jnp.sum((bounds[None, :] <= positions[:, None]).astype(jnp.int32), axis=1)


def per_device(
    tokens,
    gate_up_weight,
    down_factor_pool,
    up_factor_pool,
    segment_adapters,
    segment_tile_counts,
    adapter_pool_rows,
):
    groups = lax.axis_size("grp")
    device_shares = lax.axis_size(("tp", "cores"))
    group_index = lax.axis_index("grp")
    piece_index = lax.axis_index(("tp", "cores"))
    token_count = tokens.shape[0]
    full_width = tokens.shape[1] * device_shares
    local_hidden_width = gate_up_weight.shape[2]
    twice_rank = down_factor_pool.shape[2]
    rank_size = twice_rank // 2
    share_rows = down_factor_pool.shape[1] // device_shares
    local_count = down_factor_pool.shape[0]
    narrow = local_hidden_width // groups
    local_down_factor = down_factor_pool.reshape(
        local_count, device_shares, share_rows * twice_rank
    )
    local_up_factor = up_factor_pool.reshape(local_count, device_shares, -1)
    a_spread, b_spread = (
        lax.all_to_all(local_down_factor, ("tp", "cores"), split_axis=1, concat_axis=0, tiled=True),
        lax.all_to_all(local_up_factor, ("tp", "cores"), split_axis=1, concat_axis=0, tiled=True),
    )
    a_blocks, b_blocks = (
        lax.all_gather(a_spread, "grp", axis=1, tiled=True),
        lax.all_gather(b_spread, "grp", axis=1, tiled=True),
    )
    own_ids = lax.dynamic_index_in_dim(segment_adapters, group_index, 0, keepdims=False)
    own_slots = jnp.take(adapter_pool_rows, own_ids)
    a_chosen = jnp.take(a_blocks, own_slots, axis=0)
    b_chosen = jnp.take(b_blocks, own_slots, axis=0)
    gathered = lax.all_gather(tokens, ("tp", "cores"), axis=1, tiled=True)
    frozen_output = jnp.dot(
        gathered,
        gate_up_weight.reshape(full_width, 2 * local_hidden_width),
        preferred_element_type=jnp.float32,
    )
    frozen_output = frozen_output.reshape(token_count, 2, local_hidden_width)
    tile_count = token_count // TILE
    tile_seg = tile_segments(segment_tile_counts[0], tile_count)
    a_tiles = jnp.take(a_chosen, tile_seg, axis=0).reshape(
        tile_count, groups * share_rows, twice_rank
    )
    own_features = lax.dynamic_slice_in_dim(
        gathered.reshape(token_count, groups, device_shares, share_rows), piece_index, 1, axis=2
    )
    own_features = own_features.reshape(tile_count, TILE, groups * share_rows)
    partial_shrink = jnp.einsum(
        "tkd,tdr->tkr", own_features, a_tiles, preferred_element_type=jnp.float32
    )
    reduced_input = lax.psum(partial_shrink, ("tp", "cores")).astype(jnp.bfloat16)
    b_tiles = jnp.take(b_chosen, tile_seg, axis=0).reshape(tile_count, groups, rank_size, 2, narrow)
    gate_adapter_delta = jnp.einsum(
        "tkr,tmrw->tkmw",
        reduced_input[:, :, :rank_size],
        b_tiles[:, :, :, 0, :],
        preferred_element_type=jnp.float32,
    )
    up_adapter_delta = jnp.einsum(
        "tkr,tmrw->tkmw",
        reduced_input[:, :, rank_size:],
        b_tiles[:, :, :, 1, :],
        preferred_element_type=jnp.float32,
    )
    gate_combined = frozen_output[:, 0, :] + adapter_scale * gate_adapter_delta.reshape(
        token_count, local_hidden_width
    )
    up_combined = frozen_output[:, 1, :] + adapter_scale * up_adapter_delta.reshape(
        token_count, local_hidden_width
    )
    return (jax.nn.silu(gate_combined) * up_combined).astype(jnp.bfloat16)


def solution(mesh):
    return jax.shard_map(
        per_device,
        mesh=mesh,
        in_specs=(
            P("grp", ("tp", "cores")),
            P(None, None, ("tp", "cores")),
            P(("tp", "cores"), "grp", None),
            P(("tp", "cores"), "grp", None, None, None),
            P(),
            P("grp", None),
            P(),
        ),
        out_specs=P("grp", ("tp", "cores")),
        check_vma=False,
    )
```

profile of v0, /device:TPU:97, one launch (start us, length us, event | category | flops | bytes accessed | tf_op | source)
XLA Modules:
  0.0 831.8 jit_solution(2423148219487207486)
XLA Ops:
  6.5 4.0 reshape.205
  11.0 7.4 reduce.3
  19.2 39.0 %all_to_all.24 = bf16[64,2,4096]{2,1,0:T(2,128)(2,1)S(1)} all-to-all(bf16[64,2,4096]{2,1,0:T(2,128)(2,1)S(1)} %reshape.214), channel_id=1, replica_groups=mesh['grp'=4,'tp'=32,'cores'=2] {'tp','cores'}, dimensions={0} | all-to-all | bytes 2097152 | tf_op jit(solution)/shard_map/all_to_all | solution.py:42
  58.3 3.5 reshape.215
  61.8 10.1 %reshape.206 = bf16[1,64,16384]{2,0,1:T(2,128)(2,1)} reshape(bf16[1,1,64,128,128]{4,3,2,1,0:T(8,128)(2,1)} %param.10) | data formatting | bytes 4194304 | tf_op jit(solution)/shard_map/reshape | solution.py:40
  71.9 13.7 %reduce.2 = bf16[64,16384]{1,0:T(8,128)(2,1)S(1)} reduce(bf16[64,1,16384]{2,1,0:T(2,128)(2,1)} %bitcast.76, bf16[]{:T(256)} %broadcast.186), dimensions={1}, to_apply=%bitcast.67.reduce_sub_computation | reduce | bytes 4194306
  85.6 2.8 reshape.212
  88.4 57.5 %all_to_all.25 = bf16[64,2,8192]{2,1,0:T(2,128)(2,1)S(1)} all-to-all(bf16[64,2,8192]{2,1,0:T(2,128)(2,1)} %reshape.212), channel_id=1, replica_groups=mesh['grp'=4,'tp'=32,'cores'=2] {'tp','cores'}, dimensions={0} | all-to-all | bytes 4194304 | tf_op jit(solution)/shard_map/all_to_all | solution.py:43
  145.8 6.7 reshape.213
  153.5 8.0 copy.65
  161.5 12.2 %copy.48 = bf16[512,8192]{1,0:T(8,128)(2,1)} copy(bf16[512,8192]{0,1:T(8,128)(2,1)} %bitcast.74) | data formatting | bytes 16777216 | tf_op jit(solution)/shard_map/dot_general | solution.py:54
  174.6 27.3 %reduce = bf16[64,32768]{1,0:T(8,128)(2,1)} reduce(bf16[1,64,32768]{2,0,1:T(2,128)(2,1)} %all-gather.8.cloned.1.call-done, bf16[]{:T(256)} %constant.100), dimensions={0}, to_apply=%all-gather.reduce_sub_computation | reduce | bytes 8388610 | tf_op jit(solution)/shard_map/all_gather | solution.py:46
  201.9 7.9 reshape.198
  209.8 3.0 gather_fusion.1
  213.0 1.0 gather_fusion.2
  214.0 1.2 gather.30
  215.1 91.7 %all-gather.10.cloned.1.call-done = bf16[1,64,65536]{2,0,1:T(2,128)(2,1)} async-done(((bf16[1,64,16384]{2,0,1:T(2,128)(2,1)}), bf16[1,64,65536]{2,0,1:T(2,128)(2,1)}) %all-gather.10.cloned.1.call-update) | async-done | bytes 8388624 | tf_op jit(solution)/shard_map/all_gather | solution.py:47
  306.9 52.7 %reduce.1 = bf16[64,65536]{1,0:T(8,128)(2,1)} reduce(bf16[1,64,65536]{2,0,1:T(2,128)(2,1)} %all-gather.10.cloned.1.call-done, bf16[]{:T(256)} %constant.100), dimensions={0}, to_apply=%all-gather.1.reduce_sub_computation | reduce | bytes 16777218 | tf_op jit(solution)/shard_map/all_gather | solution.py:47
  359.5 11.7 %reshape.199 = bf16[64,4,16384]{2,1,0:T(4,128)(2,1)} reshape(bf16[64,65536]{1,0:T(8,128)(2,1)} %reduce.1) | data formatting | bytes 16777216 | tf_op jit(solution)/shard_map/all_gather | solution.py:47
  371.2 4.4 gather_fusion.3
  375.9 1.4 gather_fusion.4
  377.3 1.7 reshape.207
  379.0 1.5 copy.54
  381.6 129.9 %all-gather.6.cloned.1.call-done = bf16[1024,8192]{1,0:T(8,128)(2,1)} async-done(((bf16[1024,128]{1,0:T(8,128)(2,1)}), bf16[1024,8192]{1,0:T(8,128)(2,1)}) %all-gather.6.cloned.1.call-update) | async-done | bytes 16777232 | tf_op jit(solution)/shard_map/all_gather | solution.py:53
  511.4 22.4 %copy.49 = bf16[1024,8192]{0,1:T(8,128)(2,1)} copy(bf16[1024,8192]{1,0:T(8,128)(2,1)} %all-gather.6.cloned.1.call-done) | data formatting | bytes 33554432 | tf_op jit(solution)/shard_map/all_gather | solution.py:53
  533.9 1.0 constant_dynamic-slice_fusion.1
  535.3 266.7 %all-reduce.1 = bf16[8,128,256]{2,1,0:T(8,128)(2,1)S(1)} all-reduce(f32[8,128,256]{2,1,0:T(8,128)S(1)} %fusion.6), channel_id=1, replica_groups=mesh['grp'=4,'tp'=32,'cores'=2] {'tp','cores'}, use_global_device_ids=true, to_apply=%region_2.3 | all-reduce | flops 262144 | bytes 1572864 | tf_op jit(solution)/shard_map/psum | solution.py:72
  803.8 2.2 reshape.209
  806.0 1.4 fusion.11
  808.4 1.2 reshape.208
  809.6 14.5 %fusion = f32[1024,2,256]{2,0,1:T(8,128)S(1)} fusion(bf16[2,256,8192]{2,1,0:T(8,128)(2,1)} %bitcast.79, bf16[1024,8192]{1,0:T(8,128)(2,1)} %all-gather.6.cloned.1.call-done), kind=kOutput, calls=%fused_computation.5 | convolution fusion | flops 8589934592 | bytes 27262976 | tf_op jit(solution)/shard_map/dot_general | solution.py:54
  824.1 1.1 fusion.4
  (45 shorter events, 7.8 us)
Async XLA Ops:
  6.5 167.2 %copy-start = (s32[64]{0:T(128)S(1)}, s32[64]{0:T(128)}, u32[]{:S(2)}) copy-start(s32[64]{0:T(128)} %param.13) | copy-start | bytes 772
  6.5 168.1 %all-gather.8.cloned.1.call-start = ((), (), s32[]{:S(2)}) async-start(), calls=%async_computation.3 | async-start | bytes 10485760 | tf_op jit(solution)/shard_map/all_gather | solution.py:46
  61.8 245.1 %all-gather.10.cloned.1.call-start = ((), (), s32[]{:S(2)}) async-start(), calls=%async_computation.4 | async-start | bytes 20971520 | tf_op jit(solution)/shard_map/all_gather | solution.py:47
  88.4 65.0 %copy-start.6 = (s32[1,3]{1,0:T(1,128)S(1)}, s32[1,3]{1,0:T(1,128)}, u32[]{:S(2)}) copy-start(s32[1,3]{1,0:T(1,128)} %param.12) | copy-start | bytes 40
  152.6 358.9 %all-gather.6.cloned.1.call-start = ((), (), s32[]{:S(2)}) async-start(), calls=%async_computation.2 | async-start | bytes 17039360 | tf_op jit(solution)/shard_map/all_gather | solution.py:53
  161.5 12.2 %copy-start.5 = (s32[4,3]{1,0:T(4,128)S(1)}, s32[4,3]{1,0:T(4,128)}, u32[]{:S(2)}) copy-start(s32[4,3]{1,0:T(4,128)} %param.11) | copy-start | bytes 148
  381.6 153.3 %copy-start.4 = (bf16[8,128,256]{2,1,0:T(8,128)(2,1)S(1)}, bf16[8,128,256]{2,1,0:T(8,128)(2,1)}, u32[]{:S(2)}) copy-start(bf16[8,128,256]{2,1,0:T(8,128)(2,1)} %gather.30) | copy-start | bytes 1572868
  802.0 0.8 copy-start.3
  809.6 14.6 %copy-start.2 = (f32[1024,256]{1,0:T(8,128)S(1)}, f32[1024,256]{1,0:T(8,128)}, u32[]{:S(2)}) copy-start(f32[1024,256]{1,0:T(8,128)} %reshape.209) | copy-start | bytes 3145732
  809.6 15.7 %copy-start.1 = (s32[64]{0:T(128)S(1)}, s32[64]{0:T(128)}, u32[]{:S(2)}) copy-start(s32[64]{0:T(128)} %param.13) | copy-start | bytes 772
Sparse Core Ops, SparseCore 0:
  61.9 83.1 all-gather.7
  152.7 154.1 all-gather.9
  308.6 202.7 all-gather.5
where the time goes:
time: 834 us; the launch traced here: 832 us
  blocking collectives  363 us (44%)
  waiting for transfers between devices  222 us (27%)
  local copies, waits for them, and re-layouts  113 us (14%)
  other arithmetic  103 us (12%)
  matrix products  16.6 us (2%)
  between operations  13.4 us (2%)
    psum x1, blocking collectives, per_device(): lax.psum(partial_shrink, ('tp', 'cores')).astype(jnp.bfloat16)  267 us
    all_gather x1, waiting for transfers between devices, per_device(): gathered = lax.all_gather(tokens, ('tp', 'cores'), axis=1, tiled=True)  130 us
    all_gather x1, waiting for transfers between devices, per_device(): lax.all_gather(b_spread, 'grp', axis=1, tiled=True)  91.7 us
    all_to_all x1, blocking collectives, per_device(): lax.all_to_all(local_up_factor, ('tp', 'cores'), split_axis=1, concat_axi...  57.5 us
    all_gather x1, other arithmetic, per_device(): lax.all_gather(b_spread, 'grp', axis=1, tiled=True)  52.7 us
    all_to_all x1, blocking collectives, per_device(): lax.all_to_all(local_down_factor, ('tp', 'cores'), split_axis=1, concat_a...  39 us
    all_gather x1, other arithmetic, per_device(): lax.all_gather(a_spread, 'grp', axis=1, tiled=True)  27.3 us
    unnamed x21, local copies, waits for them, and re-layouts  22.9 us
  transfers between devices with their start and end apart: 3, of which 2 were waited for; matrix products, arithmetic and copies ran while one was open for 20% of the time, Pallas kernels for 0%

commit v1 on v0

--- a/solution.py
+++ b/solution.py
@@ -5,6 +5,11 @@
 
 TILE = 128
 adapter_scale = 0.5
+
+
+def axis_by_axis(array, inner_axis, outer_axis):
+    half = lax.psum(array, inner_axis)
+    return lax.psum(half, outer_axis)
 
 
 def tile_segments(tile_lengths, tile_count):
@@ -69,7 +74,7 @@
     partial_shrink = jnp.einsum(
         "tkd,tdr->tkr", own_features, a_tiles, preferred_element_type=jnp.float32
     )
-    reduced_input = lax.psum(partial_shrink, ("tp", "cores")).astype(jnp.bfloat16)
+    reduced_input = axis_by_axis(partial_shrink, "cores", "tp").astype(jnp.bfloat16)
     b_tiles = jnp.take(b_chosen, tile_seg, axis=0).reshape(tile_count, groups, rank_size, 2, narrow)
     gate_adapter_delta = jnp.einsum(
         "tkr,tmrw->tkmw",

time: 834 us -> 727 us (0.87)
  the two profiles are of different devices: /device:TPU:97 before, /device:TPU:2 now
where the time goes in v1:
time: 727 us; the launch traced here: 725 us
  waiting for transfers between devices  261 us (36%)
  blocking collectives  214 us (29%)
  local copies, waits for them, and re-layouts  112 us (15%)
  other arithmetic  105 us (14%)
  matrix products  18.9 us (3%)
  between operations  13.4 us (2%)
    all_gather x1, waiting for transfers between devices, per_device(): gathered = lax.all_gather(tokens, ('tp', 'cores'), axis=1, tiled=True)  129 us
    psum x1, blocking collectives, axis_by_axis(): return lax.psum(half, outer_axis)  118 us
    all_gather x1, waiting for transfers between devices, per_device(): lax.all_gather(b_spread, 'grp', axis=1, tiled=True)  94 us
    all_to_all x1, blocking collectives, per_device(): lax.all_to_all(local_up_factor, ('tp', 'cores'), split_axis=1, concat_axi...  56 us
    all_gather x1, other arithmetic, per_device(): lax.all_gather(b_spread, 'grp', axis=1, tiled=True)  52.7 us
    all_to_all x1, blocking collectives, per_device(): lax.all_to_all(local_down_factor, ('tp', 'cores'), split_axis=1, concat_a...  39.8 us
    psum x1, waiting for transfers between devices, axis_by_axis(): half = lax.psum(array, inner_axis)  37.3 us
    all_gather x1, other arithmetic, per_device(): lax.all_gather(a_spread, 'grp', axis=1, tiled=True)  27.4 us
  transfers between devices with their start and end apart: 4, of which 3 were waited for; matrix products, arithmetic and copies ran while one was open for 26% of the time, Pallas kernels for 0%

profile of v1, /device:TPU:2, one launch (start us, length us, event | category | flops | bytes accessed | tf_op | source)
XLA Modules:
  0.0 724.6 jit_solution(8085243916009657662)
XLA Ops:
  6.5 4.0 reshape.205
  11.0 7.4 %reduce.3 = bf16[64,8192]{1,0:T(8,128)(2,1)S(1)} reduce(bf16[64,1,8192]{2,1,0:T(2,128)(2,1)S(1)} %bitcast.81, bf16[]{:T(256)} %broadcast.186), dimensions={1}, to_apply=%bitcast.69.reduce_sub_computation | reduce | bytes 2097154
  19.2 39.8 %all_to_all.24 = bf16[64,2,4096]{2,1,0:T(2,128)(2,1)S(1)} all-to-all(bf16[64,2,4096]{2,1,0:T(2,128)(2,1)S(1)} %reshape.214), channel_id=1, replica_groups=mesh['grp'=4,'tp'=32,'cores'=2] {'tp','cores'}, dimensions={0} | all-to-all | bytes 2097152 | tf_op jit(solution)/shard_map/all_to_all | solution.py:47
  59.0 3.5 reshape.215
  62.5 10.1 %reshape.206 = bf16[1,64,16384]{2,0,1:T(2,128)(2,1)} reshape(bf16[1,1,64,128,128]{4,3,2,1,0:T(8,128)(2,1)} %param.10) | data formatting | bytes 4194304 | tf_op jit(solution)/shard_map/reshape | solution.py:45
  72.6 13.7 %reduce.2 = bf16[64,16384]{1,0:T(8,128)(2,1)S(1)} reduce(bf16[64,1,16384]{2,1,0:T(2,128)(2,1)} %bitcast.76, bf16[]{:T(256)} %broadcast.186), dimensions={1}, to_apply=%bitcast.67.reduce_sub_computation | reduce | bytes 4194306
  86.3 2.8 reshape.212
  89.1 56.0 %all_to_all.25 = bf16[64,2,8192]{2,1,0:T(2,128)(2,1)S(1)} all-to-all(bf16[64,2,8192]{2,1,0:T(2,128)(2,1)} %reshape.212), channel_id=1, replica_groups=mesh['grp'=4,'tp'=32,'cores'=2] {'tp','cores'}, dimensions={0} | all-to-all | bytes 4194304 | tf_op jit(solution)/shard_map/all_to_all | solution.py:48
  145.1 6.7 reshape.213
  152.8 8.0 %copy.65 = bf16[1024,8,2,256]{3,1,2,0:T(8,128)(2,1)} copy(bf16[1024,8,2,256]{3,2,1,0:T(2,128)(2,1)} %bitcast.78) | data formatting | bytes 16777216
  160.8 11.7 %copy.48 = bf16[512,8192]{1,0:T(8,128)(2,1)} copy(bf16[512,8192]{0,1:T(8,128)(2,1)} %bitcast.74) | data formatting | bytes 16777216 | tf_op jit(solution)/shard_map/dot_general | solution.py:59
  173.4 27.4 %reduce = bf16[64,32768]{1,0:T(8,128)(2,1)} reduce(bf16[1,64,32768]{2,0,1:T(2,128)(2,1)} %all-gather.8.cloned.1.call-done, bf16[]{:T(256)} %constant.100), dimensions={0}, to_apply=%all-gather.reduce_sub_computation | reduce | bytes 8388610 | tf_op jit(solution)/shard_map/all_gather | solution.py:51
  200.8 7.9 %reshape.198 = bf16[64,4,8192]{2,1,0:T(4,128)(2,1)} reshape(bf16[64,32768]{1,0:T(8,128)(2,1)} %reduce) | data formatting | bytes 8388608 | tf_op jit(solution)/shard_map/all_gather | solution.py:51
  208.6 3.0 gather_fusion.1
  212.8 1.2 gather.30
  213.9 94.0 %all-gather.10.cloned.1.call-done = bf16[1,64,65536]{2,0,1:T(2,128)(2,1)} async-done(((bf16[1,64,16384]{2,0,1:T(2,128)(2,1)}), bf16[1,64,65536]{2,0,1:T(2,128)(2,1)}) %all-gather.10.cloned.1.call-update) | async-done | bytes 8388624 | tf_op jit(solution)/shard_map/all_gather | solution.py:52
  308.0 52.7 %reduce.1 = bf16[64,65536]{1,0:T(8,128)(2,1)} reduce(bf16[1,64,65536]{2,0,1:T(2,128)(2,1)} %all-gather.10.cloned.1.call-done, bf16[]{:T(256)} %constant.100), dimensions={0}, to_apply=%all-gather.1.reduce_sub_computation | reduce | bytes 16777218 | tf_op jit(solution)/shard_map/all_gather | solution.py:52
  360.6 11.7 %reshape.199 = bf16[64,4,16384]{2,1,0:T(4,128)(2,1)} reshape(bf16[64,65536]{1,0:T(8,128)(2,1)} %reduce.1) | data formatting | bytes 16777216 | tf_op jit(solution)/shard_map/all_gather | solution.py:52
  372.3 4.4 gather_fusion.3
  377.0 1.4 gather_fusion.4
  378.4 1.7 reshape.207
  380.1 1.5 copy.54
  382.6 128.9 %all-gather.6.cloned.1.call-done = bf16[1024,8192]{1,0:T(8,128)(2,1)} async-done(((bf16[1024,128]{1,0:T(8,128)(2,1)}), bf16[1024,8192]{1,0:T(8,128)(2,1)}) %all-gather.6.cloned.1.call-update) | async-done | bytes 16777232 | tf_op jit(solution)/shard_map/all_gather | solution.py:58
  511.5 22.4 %copy.49 = bf16[1024,8192]{0,1:T(8,128)(2,1)} copy(bf16[1024,8192]{1,0:T(8,128)(2,1)} %all-gather.6.cloned.1.call-done) | data formatting | bytes 33554432 | tf_op jit(solution)/shard_map/all_gather | solution.py:58
  535.0 1.3 fusion.6
  536.3 15.8 %fusion = f32[1024,2,256]{2,0,1:T(8,128)} fusion(bf16[2,256,8192]{2,1,0:T(8,128)(2,1)} %bitcast.79, bf16[1024,8192]{1,0:T(8,128)(2,1)} %all-gather.6.cloned.1.call-done), kind=kOutput, calls=%fused_computation.5 | convolution fusion | flops 8589934592 | bytes 27262976 | tf_op jit(solution)/shard_map/dot_general | solution.py:59
  552.2 37.3 %all-reduce.3.cloned.1.call-done = f32[8,128,256]{2,1,0:T(8,128)} async-done(((f32[8,128,256]{2,1,0:T(8,128)}), f32[8,128,256]{2,1,0:T(8,128)}) %all-reduce.3.cloned.1.call-update) | async-done | bytes 1048592 | tf_op jit(solution)/shard_map/psum | solution.py:11
  589.5 118.0 %all-reduce.4 = bf16[8,128,256]{2,1,0:T(8,128)(2,1)S(1)} all-reduce(f32[8,128,256]{2,1,0:T(8,128)} %all-reduce.3.cloned.1.call-done), channel_id=1, replica_groups=mesh['grp'=4,'tp'=32,'cores'=2] {'tp'}, use_global_device_ids=true, to_apply=%region_3.4 | all-reduce | flops 262144 | bytes 1572864 | tf_op jit(solution)/shard_map/psum | solution.py:12
  709.3 2.2 reshape.209
  711.5 1.4 fusion.11
  713.9 1.2 reshape.208
  715.0 3.1 fusion.4
  (46 shorter events, 9.4 us)
Async XLA Ops:
  6.5 166.0 %copy-start = (s32[64]{0:T(128)S(1)}, s32[64]{0:T(128)}, u32[]{:S(2)}) copy-start(s32[64]{0:T(128)} %param.13) | copy-start | bytes 772
  6.5 166.8 %all-gather.8.cloned.1.call-start = ((), (), s32[]{:S(2)}) async-start(), calls=%async_computation.4 | async-start | bytes 10485760 | tf_op jit(solution)/shard_map/all_gather | solution.py:51
  62.5 245.5 %all-gather.10.cloned.1.call-start = ((), (), s32[]{:S(2)}) async-start(), calls=%async_computation.5 | async-start | bytes 20971520 | tf_op jit(solution)/shard_map/all_gather | solution.py:52
  89.1 63.5 %copy-start.5 = (s32[1,3]{1,0:T(1,128)S(1)}, s32[1,3]{1,0:T(1,128)}, u32[]{:S(2)}) copy-start(s32[1,3]{1,0:T(1,128)} %param.12) | copy-start | bytes 40
  151.8 359.7 %all-gather.6.cloned.1.call-start = ((), (), s32[]{:S(2)}) async-start(), calls=%async_computation.2 | async-start | bytes 17039360 | tf_op jit(solution)/shard_map/all_gather | solution.py:58
  152.6 436.9 %all-reduce.3.cloned.1.call-start = ((), (), s32[]{:S(2)}) async-start(), calls=%async_computation.3 | async-start | bytes 2097152 | tf_op jit(solution)/shard_map/psum | solution.py:11
  160.8 11.7 %copy-start.4 = (s32[4,3]{1,0:T(4,128)S(1)}, s32[4,3]{1,0:T(4,128)}, u32[]{:S(2)}) copy-start(s32[4,3]{1,0:T(4,128)} %param.11) | copy-start | bytes 148
  382.6 152.3 %copy-start.3 = (bf16[8,128,256]{2,1,0:T(8,128)(2,1)S(1)}, bf16[8,128,256]{2,1,0:T(8,128)(2,1)}, u32[]{:S(2)}) copy-start(bf16[8,128,256]{2,1,0:T(8,128)(2,1)} %gather.30) | copy-start | bytes 1572868
  707.5 0.8 copy-start.2
  708.4 9.7 %copy-start.1 = (s32[64]{0:T(128)S(1)}, s32[64]{0:T(128)}, u32[]{:S(2)}) copy-start(s32[64]{0:T(128)} %param.13) | copy-start | bytes 772
Sparse Core Ops, SparseCore 0:
  62.6 83.5 all-gather.7
  151.9 155.9 all-gather.9
  309.7 201.7 all-gather.5
  536.5 52.9 all-reduce.2
